TPU v7x, 512 devices: a whole 4x8x8 slice. The times are simulated.
512 devices in a mesh: dp: 64 (over y, z), factor: 8 (over x, core).
Axes of the slice: x: 4, y: 8, z: 8, core: 2. Of those that a mesh axis runs over, the one named last changes fastest.
Arguments:
- layer_inputs: bfloat16 [65536, 5120], P('dp', 'factor'), may hold values from -64 to 64
- out_grads: bfloat16 [65536, 5120], P('dp', 'factor'), may hold values from -64 to 64
- weight_grad: bfloat16 [5120, 5120], P('dp', 'factor'), may hold values from -32 to 32
- left_inv: float32 [5120, 5120], P('dp', 'factor'), may hold values from -4 to 10, as said below
- right_inv: float32 [5120, 5120], P('factor', 'dp'), may hold values from -4 to 10, as said below
Outputs:
- precond_grad: bfloat16 [5120, 5120], P('dp', 'factor')
- new_left: float32 [5120, 5120], P('dp', 'factor')
- new_right: float32 [5120, 5120], P('factor', 'dp')
Inputs may be any that keep to these rules, and one draw needn't show every extreme that they name: `left_inv`: symmetric and positive definite, every eigenvalue 0.1 or more. `right_inv`: symmetric and positive definite, every eigenvalue 0.1 or more.
All inputs are finite; a program needn't handle non-finite values.
Results may differ from a plain program's by a relative error of at most 0.00275.
The roundings to bfloat16 on the way count: a program that leaves them out, or rounds other values in their place, can miss the bound.
Values may be sent and summed in bfloat16 or wider, within the bound.
No kernel may reach another device: no remote copies, remote signals or barrier semaphores. Data moves between devices by JAX's collectives and lax.ppermute only.
A program may use at most 64 MiB of HBM per device.

v0:
```python
import jax
import jax.numpy as jnp
from jax import lax
from jax.sharding import Mesh, PartitionSpec as P

decay = 0.9
PAD = 104


def coefficient(quadratic):
    return (1.0 - decay) / (decay * decay * (1.0 + (1.0 - decay) / decay * quadratic))


def share(vec, axes, count):
    return lax.all_to_all(jnp.broadcast_to(vec[None], (count,) + vec.shape), axes, 0, 0, tiled=True)


def gather_rows(block, axis, count):
    rows, cols = block.shape
    padded = jnp.pad(block, ((0, PAD - rows), (0, 0)))
    whole = lax.all_gather(padded, axis, axis=0, tiled=False)
    return whole[:, :rows, :].reshape(count * rows, cols)


def per_device(layer_inputs, out_grads, weight_grad, left_inv, right_inv):
    ny, nz, nf = (lax.axis_size("y"), lax.axis_size("z"), lax.axis_size("f"))
    token_count = layer_inputs.shape[0] * ny * nz
    rows, cols = left_inv.shape
    y, z, f = (lax.axis_index("y"), lax.axis_index("z"), lax.axis_index("f"))
    left_wide = lax.all_gather(left_inv, "y", axis=0, tiled=True)
    swap = [(a * nf + b, b * nf + a) for a in range(ny) for b in range(nf)]
    weight_piece = lax.ppermute(weight_grad, ("y", "f"), swap)
    act_local = jnp.sum(layer_inputs, axis=0, dtype=jnp.float32)
    grad_local = jnp.sum(out_grads, axis=0, dtype=jnp.float32)
    sums = share(jnp.concatenate([act_local, grad_local]), ("y", "z"), ny * nz)
    means = jnp.sum(sums, axis=0) / token_count
    mean_act, mean_grad = (means[:cols], means[cols:])
    weight_piece, means = lax.optimization_barrier((weight_piece, means))
    weight_block = gather_rows(weight_piece, "z", nz)
    left_partial = jnp.sum(left_inv * means[None, :cols], axis=1)
    right_partial = jnp.sum(right_inv * means[cols:, None], axis=0)
    both = share(jnp.concatenate([means, left_partial, right_partial]), "f", nf)
    whole_act = both[:, :cols].reshape(nf * cols)
    whole_grad = both[:, cols : 2 * cols].reshape(nf * cols)
    images = jnp.sum(both[:, 2 * cols :], axis=0)
    all_images = share(images, ("y", "z"), ny * nz)
    left_image = all_images[:, :rows].reshape(ny * nz * rows)
    right_image = all_images[:, rows:].reshape(ny * nz * rows)
    left_coef = coefficient(jnp.sum(whole_act * left_image))
    right_coef = coefficient(jnp.sum(whole_grad * right_image))
    left_cols = lax.dynamic_slice_in_dim(left_image, f * cols, cols)
    right_rows = lax.dynamic_slice_in_dim(right_image, f * cols, cols)
    new_left = left_inv / decay - left_coef * images[:rows, None] * left_cols[None, :]
    new_right = right_inv / decay - right_coef * right_rows[:, None] * images[None, rows:]
    right_block = gather_rows(new_right.astype(jnp.bfloat16).T, "z", nz)
    wide_rows = lax.dynamic_slice_in_dim(left_image.reshape(ny, nz, rows), z, 1, 1).reshape(
        ny * rows
    )
    left_block = left_wide / decay - left_coef * wide_rows[:, None] * left_cols[None, :]
    partial = jnp.dot(
        left_block.astype(jnp.bfloat16), weight_block, preferred_element_type=jnp.float32
    )
    pieces = lax.all_to_all(partial.reshape(nf, ny * rows // nf, cols), "f", 0, 0, tiled=True)
    hidden_piece = jnp.sum(pieces, axis=0).astype(jnp.bfloat16)
    hidden = lax.all_gather(hidden_piece, "f", axis=0, tiled=True)
    partial = jnp.dot(hidden, right_block, preferred_element_type=jnp.float32)
    pieces = lax.all_to_all(partial.reshape(ny, rows, cols), "y", 0, 0, tiled=True)
    precond = jnp.sum(pieces, axis=0).astype(jnp.bfloat16)
    return (precond, new_left, new_right)


def solution(mesh):
    cube = Mesh(mesh.devices.reshape(8, 8, 8), ("y", "z", "f"))
    rows, cols = (P(("y", "z"), "f"), P("f", ("y", "z")))
    return jax.shard_map(
        per_device,
        mesh=cube,
        in_specs=(rows, rows, rows, rows, cols),
        out_specs=(rows, rows, cols),
        check_vma=False,
    )
```

profile of v0, /device:TPU:1, one launch (start us, length us, event | category | flops | bytes accessed | tf_op | source)
XLA Modules:
  0.0 244.4 jit_solution(15196800060828398383)
XLA Ops:
  7.2 2.2 convert_reduce_fusion
  9.4 0.9 broadcast_in_dim.6
  10.3 17.1 %all-to-all-start = ((f32[64,1,1280]{2,1,0:T(1,128)}), f32[64,1,1280]{2,1,0:T(1,128)S(1)}, u32[]{:S(2)}, u32[]{:S(2)}) async-start(f32[64,1,1280]{2,1,0:T(1,128)} %broadcast_in_dim.6), calls=%async_computation | async-start | bytes 655360 | tf_op jit(solution)/shard_map/all_to_all | solution.py:15
  27.4 0.0 all-gather.8.cloned.1.call-start
  27.4 4.0 %collective-permute-start = (bf16[80,640]{1,0:T(8,128)(2,1)S(1)}, bf16[80,640]{1,0:T(8,128)(2,1)S(1)}, u32[]{:S(2)}, u32[]{:S(2)}) collective-permute-start(bf16[80,640]{1,0:T(8,128)(2,1)S(1)} %copy-done.2), channel_id=1, source_target_pairs={{0,0},{1,64},{2,128},{3,192},{4,256},{5,320},{6,384},{7,448},{64,1... | collective-permute-start | bytes 307208 | tf_op jit(solution)/shard_map/ppermute | solution.py:32
  31.5 9.7 %all-to-all-done = f32[64,1,1280]{2,1,0:T(1,128)S(1)} async-done(((f32[64,1,1280]{2,1,0:T(1,128)}), f32[64,1,1280]{2,1,0:T(1,128)S(1)}, u32[]{:S(2)}, u32[]{:S(2)}) %all-to-all-start) | async-done | bytes 327712 | tf_op jit(solution)/shard_map/all_to_all | solution.py:15
  41.2 0.2 reduce_sum.92
  41.5 0.7 pad.7
  42.1 0.0 all-gather.8.cloned.1.call-update
  42.2 0.0 all-gather.6.cloned.1.call-start
  42.2 0.7 all-gather.6.cloned.1.call-update
  42.9 0.1 multiply_reduce_fusion.1
  43.1 0.1 multiply_reduce_fusion
  43.2 0.1 concatenate.7
  43.3 16.8 %all_to_all.34 = f32[8,1,1440]{2,1,0:T(1,128)S(1)} all-to-all(f32[8,1,1440]{2,1,0:T(1,128)S(1)} %broadcast_in_dim.7), channel_id=1, replica_groups=mesh['y'=8,'z'=8,'f'=8] {'f'}, dimensions={0} | all-to-all | bytes 92160 | tf_op jit(solution)/shard_map/all_to_all | solution.py:15
  60.1 0.7 broadcast_in_dim.8
  60.8 5.6 %all-to-all-start.2 = ((f32[64,1,160]{2,1,0:T(1,128)}), f32[64,1,160]{2,1,0:T(1,128)S(1)}, u32[]{:S(2)}, u32[]{:S(2)}) async-start(f32[64,1,160]{2,1,0:T(1,128)} %broadcast_in_dim.8), calls=%async_computation.2 | async-start | bytes 131072 | tf_op jit(solution)/shard_map/all_to_all | solution.py:15
  66.4 0.0 all-gather.10.cloned.1.call-start
  66.5 11.1 %all-to-all-done.2 = f32[64,1,160]{2,1,0:T(1,128)S(1)} async-done(((f32[64,1,160]{2,1,0:T(1,128)}), f32[64,1,160]{2,1,0:T(1,128)S(1)}, u32[]{:S(2)}, u32[]{:S(2)}) %all-to-all-start.2) | async-done | bytes 40992 | tf_op jit(solution)/shard_map/all_to_all | solution.py:15
  77.5 0.1 fusion.2
  77.6 0.1 reshape.66
  77.7 0.1 reshape.65
  77.8 0.1 reshape.68
  77.9 0.1 reshape.69
  78.0 0.6 fusion
  79.3 0.1 mul.116
  80.1 0.1 dynamic_slice.10
  80.1 0.1 dynamic-slice_multiply_fusion
  80.2 0.1 slice_multiply_fusion.2
  80.3 0.8 convert_bitcast_fusion
  81.1 0.7 pad.8
  81.7 0.0 all-gather.10.cloned.1.call-update
  81.8 0.0 all-gather.8.cloned.1.call-done
  81.8 1.2 slice.47
  83.0 41.1 %all-gather.6.cloned.1.call-done = f32[640,640]{1,0:T(8,128)} async-done(((f32[80,640]{1,0:T(8,128)}), f32[640,640]{1,0:T(8,128)}) %all-gather.6.cloned.1.call-update) | async-done | bytes 1638416 | tf_op jit(solution)/shard_map/all_gather | solution.py:30
  124.1 1.7 subtract_convert_fusion
  125.8 2.1 fusion.4
  127.8 9.1 %all-to-all-start.3 = ((f32[8,80,640]{2,1,0:T(8,128)}), f32[8,80,640]{2,1,0:T(8,128)S(1)}, u32[]{:S(2)}, u32[]{:S(2)}) async-start(f32[8,80,640]{2,1,0:T(8,128)} %fusion.4), calls=%async_computation.3 | async-start | bytes 3276800 | tf_op jit(solution)/shard_map/all_to_all | solution.py:63
  137.0 29.8 %all-gather.10.cloned.1.call-done = bf16[832,640]{1,0:T(8,128)(2,1)} async-done(((bf16[104,640]{1,0:T(8,128)(2,1)}), bf16[832,640]{1,0:T(8,128)(2,1)}) %all-gather.10.cloned.1.call-update) | async-done | bytes 1064976 | tf_op jit(solution)/shard_map/all_gather | solution.py:21
  166.8 1.2 slice.50
  168.0 0.0 all-to-all-done.3
  168.0 0.1 reduce_sum.97
  168.1 18.7 %all_gather.21 = bf16[640,640]{1,0:T(8,128)(2,1)S(1)} all-gather(bf16[80,640]{1,0:T(8,128)(2,1)S(1)} %reduce_sum.97), channel_id=1, replica_groups=mesh['y'=8,'z'=8,'f'=8] {'f'}, dimensions={0}, use_global_device_ids=true | all-gather | bytes 921600 | tf_op jit(solution)/shard_map/all_gather | solution.py:65
  186.8 2.1 fusion.5
  188.9 6.5 %all-to-all-start.4 = ((f32[8,80,640]{2,1,0:T(8,128)}), f32[8,80,640]{2,1,0:T(8,128)S(1)}, u32[]{:S(2)}, u32[]{:S(2)}) async-start(f32[8,80,640]{2,1,0:T(8,128)} %fusion.5), calls=%async_computation.4 | async-start | bytes 3276800 | tf_op jit(solution)/shard_map/all_to_all | solution.py:67
  195.3 0.8 multiply_subtract_fusion
  196.1 41.1 %all-to-all-done.4 = f32[8,80,640]{2,1,0:T(8,128)S(1)} async-done(((f32[8,80,640]{2,1,0:T(8,128)}), f32[8,80,640]{2,1,0:T(8,128)S(1)}, u32[]{:S(2)}, u32[]{:S(2)}) %all-to-all-start.4) | async-done | bytes 1638432 | tf_op jit(solution)/shard_map/all_to_all | solution.py:67
  237.2 0.7 reduce_sum.99
  (15 shorter events, 0.1 us)
Async XLA Ops:
  7.2 20.3 %copy-start.2 = (bf16[80,640]{1,0:T(8,128)(2,1)S(1)}, bf16[80,640]{1,0:T(8,128)(2,1)}, u32[]{:S(2)}) copy-start(bf16[80,640]{1,0:T(8,128)(2,1)} %param.7) | copy-start | bytes 307204
  7.2 35.8 %copy-start = (f32[80,640]{1,0:T(8,128)S(1)}, f32[80,640]{1,0:T(8,128)}, u32[]{:S(2)}) copy-start(f32[80,640]{1,0:T(8,128)} %param.8) | copy-start | bytes 614404
  9.4 33.7 %copy-start.1 = (f32[640,80]{0,1:T(8,128)S(1)}, f32[640,80]{0,1:T(8,128)}, u32[]{:S(2)}) copy-start(f32[640,80]{0,1:T(8,128)} %param.9) | copy-start | bytes 614404
  10.3 31.0 %all-to-all-start = ((f32[64,1,1280]{2,1,0:T(1,128)}), f32[64,1,1280]{2,1,0:T(1,128)S(1)}, u32[]{:S(2)}, u32[]{:S(2)}) async-start(f32[64,1,1280]{2,1,0:T(1,128)} %broadcast_in_dim.6), calls=%async_computation | async-start | bytes 655360 | tf_op jit(solution)/shard_map/all_to_all | solution.py:15
  27.4 54.4 %all-gather.8.cloned.1.call-start = ((), (), s32[]{:S(2)}) async-start(), calls=%async_computation.6 | async-start | bytes 1198080 | tf_op jit(solution)/shard_map/all_gather | solution.py:21
  27.4 14.0 %collective-permute-start = (bf16[80,640]{1,0:T(8,128)(2,1)S(1)}, bf16[80,640]{1,0:T(8,128)(2,1)S(1)}, u32[]{:S(2)}, u32[]{:S(2)}) collective-permute-start(bf16[80,640]{1,0:T(8,128)(2,1)S(1)} %copy-done.2), channel_id=1, source_target_pairs={{0,0},{1,64},{2,128},{3,192},{4,256},{5,320},{6,384},{7,448},{64,1... | collective-permute-start | bytes 307208 | tf_op jit(solution)/shard_map/ppermute | solution.py:32
  42.2 81.9 %all-gather.6.cloned.1.call-start = ((), (), s32[]{:S(2)}) async-start(), calls=%async_computation.5 | async-start | bytes 1843200 | tf_op jit(solution)/shard_map/all_gather | solution.py:30
  60.8 16.8 %all-to-all-start.2 = ((f32[64,1,160]{2,1,0:T(1,128)}), f32[64,1,160]{2,1,0:T(1,128)S(1)}, u32[]{:S(2)}, u32[]{:S(2)}) async-start(f32[64,1,160]{2,1,0:T(1,128)} %broadcast_in_dim.8), calls=%async_computation.2 | async-start | bytes 131072 | tf_op jit(solution)/shard_map/all_to_all | solution.py:15
  66.4 100.3 %all-gather.10.cloned.1.call-start = ((), (), s32[]{:S(2)}) async-start(), calls=%async_computation.7 | async-start | bytes 1198080 | tf_op jit(solution)/shard_map/all_gather | solution.py:21
  127.8 40.1 %all-to-all-start.3 = ((f32[8,80,640]{2,1,0:T(8,128)}), f32[8,80,640]{2,1,0:T(8,128)S(1)}, u32[]{:S(2)}, u32[]{:S(2)}) async-start(f32[8,80,640]{2,1,0:T(8,128)} %fusion.4), calls=%async_computation.3 | async-start | bytes 3276800 | tf_op jit(solution)/shard_map/all_to_all | solution.py:63
  188.9 48.3 %all-to-all-start.4 = ((f32[8,80,640]{2,1,0:T(8,128)}), f32[8,80,640]{2,1,0:T(8,128)S(1)}, u32[]{:S(2)}, u32[]{:S(2)}) async-start(f32[8,80,640]{2,1,0:T(8,128)} %fusion.5), calls=%async_computation.4 | async-start | bytes 3276800 | tf_op jit(solution)/shard_map/all_to_all | solution.py:67
Sparse Core Ops, SparseCore 0:
  42.3 38.8 all-gather.7
  83.2 40.7 all-gather.5
  126.2 40.5 all-gather.9
where the time goes:
time: 245 us; the launch traced here: 244 us
  waiting for transfers between devices  134 us (55%)
  starting transfers between devices  42.5 us (17%)
  blocking collectives  35.5 us (14%)
  between operations  15.3 us (6%)
  other arithmetic  7.46 us (3%)
  local copies, waits for them, and re-layouts  6 us (2%)
  matrix products  4.14 us (2%)
    all_to_all x1, waiting for transfers between devices, per_device(): lax.all_to_all(partial.reshape(ny, rows, cols), 'y', 0, 0, tiled=True)  41.1 us
    all_gather x1, waiting for transfers between devices, per_device(): left_wide = lax.all_gather(left_inv, 'y', axis=0, tiled=True)  41.1 us
    all_gather x2, waiting for transfers between devices, gather_rows(): whole = lax.all_gather(padded, axis, axis=0, tiled=False)  29.8 us
    all_to_all x2, starting transfers between devices, share(): lax.all_to_all(jnp.broadcast_to(vec[None], (count,) + vec.shape), axes, 0...  22.8 us
    all_to_all x2, waiting for transfers between devices, share(): lax.all_to_all(jnp.broadcast_to(vec[None], (count,) + vec.shape), axes, 0...  20.8 us
    all_gather x1, blocking collectives, per_device(): hidden = lax.all_gather(hidden_piece, 'f', axis=0, tiled=True)  18.7 us
    all_to_all x1, blocking collectives, share(): lax.all_to_all(jnp.broadcast_to(vec[None], (count,) + vec.shape), axes, 0...  16.8 us
    all_to_all x1, starting transfers between devices, per_device(): lax.all_to_all(partial.reshape(nf, ny * rows // nf, cols), 'f', 0, 0, til...  9.13 us
  transfers between devices with their start and end apart: 8, of which 5 were waited for; matrix products, arithmetic and copies ran while one was open for 4% of the time, Pallas kernels for 0%

commit v1 on v0

--- a/solution.py
+++ b/solution.py
@@ -62,7 +62,9 @@
     )
     pieces = lax.all_to_all(partial.reshape(nf, ny * rows // nf, cols), "f", 0, 0, tiled=True)
     hidden_piece = jnp.sum(pieces, axis=0).astype(jnp.bfloat16)
-    hidden = lax.all_gather(hidden_piece, "f", axis=0, tiled=True)
+    hidden = jnp.concatenate(
+        lax.all_to_all(jnp.stack([hidden_piece] * lax.axis_size("f")), "f", 0, 0), axis=0
+    )
     partial = jnp.dot(hidden, right_block, preferred_element_type=jnp.float32)
     pieces = lax.all_to_all(partial.reshape(ny, rows, cols), "y", 0, 0, tiled=True)
     precond = jnp.sum(pieces, axis=0).astype(jnp.bfloat16)

time: 245 us -> 235 us (0.959); the launches traced: 244 us -> 231 us
  blocking collectives: 35.5 us -> 16.8 us
  starting transfers between devices: 42.5 us -> 47.5 us
    all_to_all x1, waiting for transfers between devices: 0.01 us -> 19.7 us  [per_device(): lax.all_to_all(partial.reshape(nf, ny * rows // nf, cols), 'f', 0, 0, til...]
    all_gather x1 -> x0, blocking collectives: 18.7 us -> none  [per_device(): hidden = lax.all_gather(hidden_piece, 'f', axis=0, tiled=True)]
    all_gather x2, waiting for transfers between devices: 29.8 us -> 13.1 us  [gather_rows(): whole = lax.all_gather(padded, axis, axis=0, tiled=False)]
    all_to_all x0 -> x1, starting transfers between devices: none -> 4.42 us  [per_device(): lax.all_to_all(jnp.stack([hidden_piece] * lax.axis_size('f')), 'f', 0, 0)]
    all_to_all x1, waiting for transfers between devices: 41.1 us -> 37.1 us  [per_device(): lax.all_to_all(partial.reshape(ny, rows, cols), 'y', 0, 0, tiled=True)]
  transfers between devices with their start and end apart: 8 -> 9, of which waited for: 5 -> 7; matrix products, arithmetic and copies ran while one was open for 4% -> 4% of each run, Pallas kernels for 0% -> 0%
where the time goes in v1:
time: 235 us; the launch traced here: 231 us
  waiting for transfers between devices  133 us (57%)
  starting transfers between devices  47.5 us (20%)
  blocking collectives  16.8 us (7%)
  between operations  15.3 us (7%)
  other arithmetic  7.46 us (3%)
  local copies, waits for them, and re-layouts  6.95 us (3%)
  matrix products  4.15 us (2%)
    all_gather x1, waiting for transfers between devices, per_device(): left_wide = lax.all_gather(left_inv, 'y', axis=0, tiled=True)  41.7 us
    all_to_all x1, waiting for transfers between devices, per_device(): lax.all_to_all(partial.reshape(ny, rows, cols), 'y', 0, 0, tiled=True)  37.1 us
    all_to_all x2, starting transfers between devices, share(): lax.all_to_all(jnp.broadcast_to(vec[None], (count,) + vec.shape), axes, 0...  22.8 us
    all_to_all x2, waiting for transfers between devices, share(): lax.all_to_all(jnp.broadcast_to(vec[None], (count,) + vec.shape), axes, 0...  20.9 us
    all_to_all x1, waiting for transfers between devices, per_device(): lax.all_to_all(partial.reshape(nf, ny * rows // nf, cols), 'f', 0, 0, til...  19.7 us
    all_to_all x1, blocking collectives, share(): lax.all_to_all(jnp.broadcast_to(vec[None], (count,) + vec.shape), axes, 0...  16.8 us
    all_gather x2, waiting for transfers between devices, gather_rows(): whole = lax.all_gather(padded, axis, axis=0, tiled=False)  13.1 us
    all_to_all x1, starting transfers between devices, per_device(): lax.all_to_all(partial.reshape(nf, ny * rows // nf, cols), 'f', 0, 0, til...  9.13 us
  transfers between devices with their start and end apart: 9, of which 7 were waited for; matrix products, arithmetic and copies ran while one was open for 4% of the time, Pallas kernels for 0%

profile of v1, /device:TPU:1, one launch (start us, length us, event | category | flops | bytes accessed | tf_op | source)
XLA Modules:
  0.0 231.4 jit_solution(16084451471756805442)
XLA Ops:
  7.2 2.2 convert_reduce_fusion
  9.4 0.9 broadcast_in_dim.6
  10.3 17.1 %all-to-all-start = ((f32[64,1,1280]{2,1,0:T(1,128)}), f32[64,1,1280]{2,1,0:T(1,128)S(1)}, u32[]{:S(2)}, u32[]{:S(2)}) async-start(f32[64,1,1280]{2,1,0:T(1,128)} %broadcast_in_dim.6), calls=%async_computation | async-start | bytes 655360 | tf_op jit(solution)/shard_map/all_to_all | solution.py:15
  27.4 0.0 all-gather.8.cloned.1.call-start
  27.4 4.0 %collective-permute-start = (bf16[80,640]{1,0:T(8,128)(2,1)S(1)}, bf16[80,640]{1,0:T(8,128)(2,1)S(1)}, u32[]{:S(2)}, u32[]{:S(2)}) collective-permute-start(bf16[80,640]{1,0:T(8,128)(2,1)S(1)} %copy-done.2), channel_id=1, source_target_pairs={{0,0},{1,64},{2,128},{3,192},{4,256},{5,320},{6,384},{7,448},{64,1... | collective-permute-start | bytes 307208 | tf_op jit(solution)/shard_map/ppermute | solution.py:32
  31.5 9.7 %all-to-all-done = f32[64,1,1280]{2,1,0:T(1,128)S(1)} async-done(((f32[64,1,1280]{2,1,0:T(1,128)}), f32[64,1,1280]{2,1,0:T(1,128)S(1)}, u32[]{:S(2)}, u32[]{:S(2)}) %all-to-all-start) | async-done | bytes 327712 | tf_op jit(solution)/shard_map/all_to_all | solution.py:15
  41.2 0.2 reduce_sum.92
  41.5 0.7 pad.7
  42.1 0.0 all-gather.8.cloned.1.call-update
  42.2 0.0 all-gather.6.cloned.1.call-start
  42.2 0.7 all-gather.6.cloned.1.call-update
  42.9 0.1 multiply_reduce_fusion.1
  43.1 0.1 multiply_reduce_fusion
  43.2 0.1 concatenate.7
  43.3 16.8 %all_to_all.39 = f32[8,1,1440]{2,1,0:T(1,128)S(1)} all-to-all(f32[8,1,1440]{2,1,0:T(1,128)S(1)} %broadcast_in_dim.7), channel_id=1, replica_groups=mesh['y'=8,'z'=8,'f'=8] {'f'}, dimensions={0} | all-to-all | bytes 92160 | tf_op jit(solution)/shard_map/all_to_all | solution.py:15
  60.1 0.7 broadcast_in_dim.8
  60.8 5.6 %all-to-all-start.2 = ((f32[64,1,160]{2,1,0:T(1,128)}), f32[64,1,160]{2,1,0:T(1,128)S(1)}, u32[]{:S(2)}, u32[]{:S(2)}) async-start(f32[64,1,160]{2,1,0:T(1,128)} %broadcast_in_dim.8), calls=%async_computation.2 | async-start | bytes 131072 | tf_op jit(solution)/shard_map/all_to_all | solution.py:15
  66.4 11.1 %all-to-all-done.2 = f32[64,1,160]{2,1,0:T(1,128)S(1)} async-done(((f32[64,1,160]{2,1,0:T(1,128)}), f32[64,1,160]{2,1,0:T(1,128)S(1)}, u32[]{:S(2)}, u32[]{:S(2)}) %all-to-all-start.2) | async-done | bytes 40992 | tf_op jit(solution)/shard_map/all_to_all | solution.py:15
  77.5 0.1 fusion.2
  77.6 0.1 reshape.70
  77.7 0.1 reshape.69
  77.8 0.1 reshape.72
  77.9 0.1 reshape.73
  78.0 0.6 fusion
  79.3 0.1 mul.116
  80.1 0.1 dynamic_slice.10
  80.1 0.1 slice_multiply_fusion.2
  80.2 0.9 all-gather.8.cloned.1.call-done
  81.2 1.2 slice.47
  82.4 41.7 %all-gather.6.cloned.1.call-done = f32[640,640]{1,0:T(8,128)} async-done(((f32[80,640]{1,0:T(8,128)}), f32[640,640]{1,0:T(8,128)}) %all-gather.6.cloned.1.call-update) | async-done | bytes 1638416 | tf_op jit(solution)/shard_map/all_gather | solution.py:30
  124.1 1.7 subtract_convert_fusion
  125.8 2.1 fusion.4
  127.8 9.1 %all-to-all-start.3 = ((f32[8,80,640]{2,1,0:T(8,128)}), f32[8,80,640]{2,1,0:T(8,128)S(1)}, u32[]{:S(2)}, u32[]{:S(2)}) async-start(f32[8,80,640]{2,1,0:T(8,128)} %fusion.4), calls=%async_computation.3 | async-start | bytes 3276800 | tf_op jit(solution)/shard_map/all_to_all | solution.py:63
  137.0 0.1 dynamic-slice_multiply_fusion
  137.0 0.8 convert_bitcast_fusion
  137.8 0.7 pad.8
  138.5 0.0 all-gather.10.cloned.1.call-update
  138.5 19.7 %all-to-all-done.3 = f32[8,80,640]{2,1,0:T(8,128)S(1)} async-done(((f32[8,80,640]{2,1,0:T(8,128)}), f32[8,80,640]{2,1,0:T(8,128)S(1)}, u32[]{:S(2)}, u32[]{:S(2)}) %all-to-all-start.3) | async-done | bytes 1638432 | tf_op jit(solution)/shard_map/all_to_all | solution.py:63
  158.3 0.1 reduce_sum.97
  158.3 1.0 stack.2
  159.3 4.4 %all-to-all-start.4 = ((bf16[8,80,640]{2,1,0:T(8,128)(2,1)}), bf16[8,80,640]{2,1,0:T(8,128)(2,1)S(1)}, u32[]{:S(2)}, u32[]{:S(2)}) async-start(bf16[8,80,640]{2,1,0:T(8,128)(2,1)} %stack.2), calls=%async_computation.4 | async-start | bytes 1638400 | tf_op jit(solution)/shard_map/all_to_all | solution.py:66
  163.7 12.2 %all-gather.10.cloned.1.call-done = bf16[832,640]{1,0:T(8,128)(2,1)} async-done(((bf16[104,640]{1,0:T(8,128)(2,1)}), bf16[832,640]{1,0:T(8,128)(2,1)}) %all-gather.10.cloned.1.call-update) | async-done | bytes 1064976 | tf_op jit(solution)/shard_map/all_gather | solution.py:21
  175.9 1.2 slice.50
  177.1 2.1 fusion.5
  179.2 7.0 %all-to-all-start.5 = ((f32[8,80,640]{2,1,0:T(8,128)}), f32[8,80,640]{2,1,0:T(8,128)S(1)}, u32[]{:S(2)}, u32[]{:S(2)}) async-start(f32[8,80,640]{2,1,0:T(8,128)} %fusion.5), calls=%async_computation.5 | async-start | bytes 3276800 | tf_op jit(solution)/shard_map/all_to_all | solution.py:69
  186.3 0.8 multiply_subtract_fusion
  187.0 37.1 %all-to-all-done.5 = f32[8,80,640]{2,1,0:T(8,128)S(1)} async-done(((f32[8,80,640]{2,1,0:T(8,128)}), f32[8,80,640]{2,1,0:T(8,128)S(1)}, u32[]{:S(2)}, u32[]{:S(2)}) %all-to-all-start.5) | async-done | bytes 1638432 | tf_op jit(solution)/shard_map/all_to_all | solution.py:69
  224.1 0.7 reduce_sum.99
  (17 shorter events, 0.1 us)
Async XLA Ops:
  7.2 20.3 %copy-start.2 = (bf16[80,640]{1,0:T(8,128)(2,1)S(1)}, bf16[80,640]{1,0:T(8,128)(2,1)}, u32[]{:S(2)}) copy-start(bf16[80,640]{1,0:T(8,128)(2,1)} %param.7) | copy-start | bytes 307204
  7.2 35.8 %copy-start = (f32[80,640]{1,0:T(8,128)S(1)}, f32[80,640]{1,0:T(8,128)}, u32[]{:S(2)}) copy-start(f32[80,640]{1,0:T(8,128)} %param.8) | copy-start | bytes 614404
  9.4 33.7 %copy-start.1 = (f32[640,80]{0,1:T(8,128)S(1)}, f32[640,80]{0,1:T(8,128)}, u32[]{:S(2)}) copy-start(f32[640,80]{0,1:T(8,128)} %param.9) | copy-start | bytes 614404
  10.3 31.0 %all-to-all-start = ((f32[64,1,1280]{2,1,0:T(1,128)}), f32[64,1,1280]{2,1,0:T(1,128)S(1)}, u32[]{:S(2)}, u32[]{:S(2)}) async-start(f32[64,1,1280]{2,1,0:T(1,128)} %broadcast_in_dim.6), calls=%async_computation | async-start | bytes 655360 | tf_op jit(solution)/shard_map/all_to_all | solution.py:15
  27.4 53.8 %all-gather.8.cloned.1.call-start = ((), (), s32[]{:S(2)}) async-start(), calls=%async_computation.7 | async-start | bytes 1198080 | tf_op jit(solution)/shard_map/all_gather | solution.py:21
  27.4 14.0 %collective-permute-start = (bf16[80,640]{1,0:T(8,128)(2,1)S(1)}, bf16[80,640]{1,0:T(8,128)(2,1)S(1)}, u32[]{:S(2)}, u32[]{:S(2)}) collective-permute-start(bf16[80,640]{1,0:T(8,128)(2,1)S(1)} %copy-done.2), channel_id=1, source_target_pairs={{0,0},{1,64},{2,128},{3,192},{4,256},{5,320},{6,384},{7,448},{64,1... | collective-permute-start | bytes 307208 | tf_op jit(solution)/shard_map/ppermute | solution.py:32
  42.2 81.9 %all-gather.6.cloned.1.call-start = ((), (), s32[]{:S(2)}) async-start(), calls=%async_computation.6 | async-start | bytes 1843200 | tf_op jit(solution)/shard_map/all_gather | solution.py:30
  60.8 16.8 %all-to-all-start.2 = ((f32[64,1,160]{2,1,0:T(1,128)}), f32[64,1,160]{2,1,0:T(1,128)S(1)}, u32[]{:S(2)}, u32[]{:S(2)}) async-start(f32[64,1,160]{2,1,0:T(1,128)} %broadcast_in_dim.8), calls=%async_computation.2 | async-start | bytes 131072 | tf_op jit(solution)/shard_map/all_to_all | solution.py:15
  127.8 30.4 %all-to-all-start.3 = ((f32[8,80,640]{2,1,0:T(8,128)}), f32[8,80,640]{2,1,0:T(8,128)S(1)}, u32[]{:S(2)}, u32[]{:S(2)}) async-start(f32[8,80,640]{2,1,0:T(8,128)} %fusion.4), calls=%async_computation.3 | async-start | bytes 3276800 | tf_op jit(solution)/shard_map/all_to_all | solution.py:63
  137.0 38.9 %all-gather.10.cloned.1.call-start = ((), (), s32[]{:S(2)}) async-start(), calls=%async_computation.8 | async-start | bytes 1198080 | tf_op jit(solution)/shard_map/all_gather | solution.py:21
  159.3 17.8 %all-to-all-start.4 = ((bf16[8,80,640]{2,1,0:T(8,128)(2,1)}), bf16[8,80,640]{2,1,0:T(8,128)(2,1)S(1)}, u32[]{:S(2)}, u32[]{:S(2)}) async-start(bf16[8,80,640]{2,1,0:T(8,128)(2,1)} %stack.2), calls=%async_computation.4 | async-start | bytes 1638400 | tf_op jit(solution)/shard_map/all_to_all | solution.py:66
  179.2 44.9 %all-to-all-start.5 = ((f32[8,80,640]{2,1,0:T(8,128)}), f32[8,80,640]{2,1,0:T(8,128)S(1)}, u32[]{:S(2)}, u32[]{:S(2)}) async-start(f32[8,80,640]{2,1,0:T(8,128)} %fusion.5), calls=%async_computation.5 | async-start | bytes 3276800 | tf_op jit(solution)/shard_map/all_to_all | solution.py:69
Sparse Core Ops, SparseCore 0:
  42.3 38.8 all-gather.7
  83.2 40.7 all-gather.5
  140.4 35.4 all-gather.9
